TPU v7x, 256 devices: a whole 4x4x8 slice. The times are simulated.
256 devices in a mesh: req: 64 (over z, x, core), tp: 4 (over y).
Axes of the slice: x: 4, y: 4, z: 8, core: 2. Of those that a mesh axis runs over, the one named last changes fastest.
Arguments:
- tokens: bfloat16 [16384, 2048], P('req'), may hold values from -6 to 6
- segment_ids: int32 [16384], P('req'), may hold values from 0 to 15, never falling along the last dimension, each value on 1 to 8192 neighbouring positions
- mixer_gain: float32 [2048], replicated, may hold values from 0.1 to 1.9
- query_weight: bfloat16 [2048, 2048], P(None, 'tp'), may hold values from -0.5 to 0.5
- pair_weight: bfloat16 [2048, 512], P(None, 'tp'), may hold values from -3 to 3
- output_weight: bfloat16 [2048, 2048], P('tp'), may hold values from -0.125 to 0.125
- feed_gain: float32 [2048], replicated, may hold values from 0.1 to 1.9
- gate_weight: bfloat16 [2048, 2048], P(None, 'tp'), may hold values from -0.125 to 0.125
- up_weight: bfloat16 [2048, 2048], P(None, 'tp'), may hold values from -0.125 to 0.125
- down_weight: bfloat16 [2048, 2048], P('tp'), may hold values from -0.125 to 0.125
Outputs:
- block_output: bfloat16 [16384, 2048], P('req')
- key_values: bfloat16 [16384, 512], P('req', 'tp')
All inputs are finite; a program needn't handle non-finite values.
Results may differ from a plain program's by a relative error of at most 0.015.
The roundings to bfloat16 on the way count: a program that leaves them out, or rounds other values in their place, can miss the bound.
Values may be sent and summed in bfloat16 or wider, within the bound.
A program may use at most 128 MiB of HBM per device.

v0:
```python
import math

import jax
import jax.numpy as jnp
from jax import lax
from jax.sharding import PartitionSpec as P

HD = 64
WINDOW = 2048


epsilon = 1e-05


def passed_along(x, axis, by):
    length = lax.axis_size(axis)
    pairs = [(i, i + by) for i in range(length) if 0 <= i + by < length]
    return lax.ppermute(x, axis, pairs)


def rms_scale(matrix, gain):
    matrix = matrix.astype(jnp.float32)
    mean_square = jnp.mean(matrix * matrix, axis=-1, keepdims=True)
    return matrix * lax.rsqrt(mean_square + epsilon) * gain


def rotary(head_data, position):
    half_width = head_data.shape[-1] // 2
    frequency = jnp.exp(-math.log(10000.0) * jnp.arange(half_width, dtype=jnp.float32) / half_width)
    angles = position.astype(jnp.float32)[:, None] * frequency[None, :]
    cosine = jnp.cos(angles)[:, None, :]
    sine_part = jnp.sin(angles)[:, None, :]
    front_half = head_data[..., :half_width]
    back_half = head_data[..., half_width:]
    return jnp.concatenate(
        [front_half * cosine - back_half * sine_part, back_half * cosine + front_half * sine_part],
        axis=-1,
    )


def body(
    tokens,
    segment_ids,
    mixer_gain,
    query_weight,
    pair_weight,
    output_weight,
    feed_gain,
    gate_weight,
    up_weight,
    down_weight,
):
    tok_rows = tokens.shape[0]
    offset = lax.axis_index("req") * tok_rows
    position = offset + jnp.arange(tok_rows, dtype=jnp.int32)
    seg_count = max(lax.axis_size("req") // 4, 4)
    segment_list = jnp.arange(seg_count, dtype=jnp.int32)
    sentinel = tok_rows * lax.axis_size("req")
    local_first = jnp.min(
        jnp.where(segment_ids[None, :] == segment_list[:, None], position[None, :], sentinel),
        axis=1,
    )
    firsts = lax.pmin(local_first, "req")
    starts = jnp.sum(
        jnp.where(segment_ids[:, None] == segment_list[None, :], firsts[None, :], 0), axis=1
    )
    normed = rms_scale(tokens, mixer_gain).astype(jnp.bfloat16)
    heads_here = query_weight.shape[1] // HD
    kv_here = pair_weight.shape[1] // (2 * HD)
    queries = jnp.dot(normed, query_weight, preferred_element_type=jnp.float32).reshape(
        tok_rows, heads_here, HD
    )
    queries = rotary(queries, position).astype(jnp.bfloat16)
    pair_rows = jnp.dot(normed, pair_weight, preferred_element_type=jnp.float32).reshape(
        tok_rows, kv_here, 2, HD
    )
    rotated_keys = rotary(pair_rows[:, :, 0], position)
    key_values = (
        jnp.stack([rotated_keys, pair_rows[:, :, 1]], axis=2)
        .astype(jnp.bfloat16)
        .reshape(tok_rows, kv_here * 2 * HD)
    )
    hop_count = WINDOW // tok_rows
    earlier = [passed_along(key_values, "req", distance) for distance in range(hop_count, 0, -1)]
    window = jnp.concatenate(earlier + [key_values], axis=0)
    key_count = window.shape[0]
    pairs = window.reshape(key_count, kv_here, 2, HD)
    grouped = queries.reshape(tok_rows, kv_here, heads_here // kv_here, HD)
    key_position = offset - WINDOW + jnp.arange(key_count, dtype=jnp.int32)
    scores = jnp.einsum(
        "qcgd,kcd->cgqk", grouped, pairs[:, :, 0], preferred_element_type=jnp.float32
    ) * HD ** (-0.5)
    allowed = (
        (key_position[None, :] >= starts[:, None])
        & (key_position[None, :] <= position[:, None])
        & (key_position[None, :] > position[:, None] - WINDOW)
    )
    scores = jnp.where(allowed[None, None], scores, -jnp.inf)
    row_max = jnp.max(scores, axis=-1, keepdims=True)
    weights = jnp.exp(scores - row_max)
    weights = (weights / jnp.sum(weights, axis=-1, keepdims=True)).astype(jnp.bfloat16)
    mixed_heads = jnp.einsum(
        "cgqk,kcd->qcgd", weights, pairs[:, :, 1], preferred_element_type=jnp.float32
    )
    mixed_heads = mixed_heads.reshape(tok_rows, heads_here * HD).astype(jnp.bfloat16)
    partial_value = jnp.dot(mixed_heads, output_weight, preferred_element_type=jnp.float32)
    attention = lax.psum(partial_value.astype(jnp.bfloat16), "tp").astype(jnp.float32)
    residual = tokens.astype(jnp.float32) + attention
    normed_mid = rms_scale(residual, feed_gain).astype(jnp.bfloat16)
    gate_rows = jnp.dot(normed_mid, gate_weight, preferred_element_type=jnp.float32)
    up_rows = jnp.dot(normed_mid, up_weight, preferred_element_type=jnp.float32)
    hidden = (jax.nn.silu(gate_rows) * up_rows).astype(jnp.bfloat16)
    feed_out = lax.psum(
        jnp.dot(hidden, down_weight, preferred_element_type=jnp.float32).astype(jnp.bfloat16), "tp"
    ).astype(jnp.float32)
    block_output = (residual + feed_out).astype(jnp.bfloat16)
    return (block_output, key_values)


def solution(mesh):
    return jax.shard_map(
        body,
        mesh=mesh,
        in_specs=(
            P("req", None),
            P("req"),
            P(),
            P(None, "tp"),
            P(None, "tp"),
            P("tp", None),
            P(),
            P(None, "tp"),
            P(None, "tp"),
            P("tp", None),
        ),
        out_specs=(P("req", None), P("req", "tp")),
        check_vma=False,
    )
```

profile of v0, /device:TPU:2, one launch (start us, length us, event | category | flops | bytes accessed | tf_op | source)
XLA Modules:
  0.0 230.0 jit_solution(1501198905631042342)
XLA Ops:
  7.3 1.7 fusion.4
  8.9 1.9 fusion.18
  11.0 0.2 fusion.29
  11.2 1.9 collective-permute-start.7
  13.1 3.4 %collective-permute-start.6 = (bf16[256,128]{0,1:T(8,128)(2,1)S(1)}, bf16[256,128]{0,1:T(8,128)(2,1)S(1)}, u32[]{:S(2)}, u32[]{:S(2)}) collective-permute-start(bf16[256,128]{0,1:T(8,128)(2,1)S(1)} %bitcast.61), channel_id=1, source_target_pairs={{0,8},{4,12},{8,16},{12,20},{16,24},{20,28},{24,32},{28,36},{32,40... | collective-permute-start | bytes 196616 | tf_op jit(solution)/shard_map/ppermute | solution.py:18
  16.5 4.4 %collective-permute-start.5 = (bf16[256,128]{0,1:T(8,128)(2,1)S(1)}, bf16[256,128]{0,1:T(8,128)(2,1)S(1)}, u32[]{:S(2)}, u32[]{:S(2)}) collective-permute-start(bf16[256,128]{0,1:T(8,128)(2,1)S(1)} %bitcast.62), channel_id=1, source_target_pairs={{0,12},{4,16},{8,20},{12,24},{16,28},{20,32},{24,36},{28,40},{32,4... | collective-permute-start | bytes 196616 | tf_op jit(solution)/shard_map/ppermute | solution.py:18
  20.9 4.9 %collective-permute-start.4 = (bf16[256,128]{0,1:T(8,128)(2,1)S(1)}, bf16[256,128]{0,1:T(8,128)(2,1)}, u32[]{:S(2)}, u32[]{:S(2)}) collective-permute-start(bf16[256,128]{0,1:T(8,128)(2,1)S(1)} %bitcast.63), channel_id=1, source_target_pairs={{0,16},{4,20},{8,24},{12,28},{16,32},{20,36},{24,40},{28,44},{32,4... | collective-permute-start | bytes 196616 | tf_op jit(solution)/shard_map/ppermute | solution.py:18
  25.8 3.8 %collective-permute-start = (bf16[256,128]{0,1:T(8,128)(2,1)S(1)}, bf16[256,128]{0,1:T(8,128)(2,1)}, u32[]{:S(2)}, u32[]{:S(2)}) collective-permute-start(bf16[256,128]{0,1:T(8,128)(2,1)S(1)} %bitcast.64), channel_id=1, source_target_pairs={{0,32},{4,36},{8,40},{12,44},{16,48},{20,52},{24,56},{28,60},{32,6... | collective-permute-start | bytes 196616 | tf_op jit(solution)/shard_map/ppermute | solution.py:18
  29.7 0.2 multiply_cosine_fusion
  30.0 17.4 %pmin.7 = s32[16]{0:T(128)} all-reduce(s32[16]{0:T(128)S(1)} %select_reduce_fusion.1), channel_id=1, replica_groups=mesh['req'=64,'tp'=4] {'req'}, use_global_device_ids=true, to_apply=%region_2.3 | all-reduce | flops 16 | bytes 128 | tf_op jit(solution)/shard_map/pmin | solution.py:63
  47.4 0.7 select_reduce_fusion
  48.2 2.6 %fusion.16 = f32[256,512]{0,1:T(8,128)S(1)} fusion(bf16[2048,512]{1,0:T(8,128)(2,1)} %param.13, bf16[256,2048]{1,0:T(8,128)(2,1)S(1)} %copy-done.1, f32[2048]{0:T(1024)} %param.12, f32[256]{0:T(256)} %copy-done.6), kind=kOutput, calls=%fused_computation.27 | convolution fusion | flops 538968064 | bytes 3679232 | tf_op jit(solution)/shard_map/dot_general | solution.py:70
  50.8 1.1 compare_and_fusion
  52.1 1.3 collective-permute-start.1
  53.4 0.8 constant_dynamic-update-slice_fusion.8
  54.2 1.0 collective-permute-done.1
  55.2 7.5 %collective-permute-start.2 = (bf16[256,128]{0,1:T(8,128)(2,1)S(1)}, bf16[256,128]{0,1:T(8,128)(2,1)S(1)}, u32[]{:S(2)}, u32[]{:S(2)}) collective-permute-start(bf16[256,128]{0,1:T(8,128)(2,1)S(1)} %bitcast.66), channel_id=1, source_target_pairs={{0,24},{4,28},{8,32},{12,36},{16,40},{20,44},{24,48},{28,52},{32,5... | collective-permute-start | bytes 196616 | tf_op jit(solution)/shard_map/ppermute | solution.py:18
  62.8 1.9 collective-permute-done.2
  64.6 3.5 %collective-permute-start.3 = (bf16[256,128]{0,1:T(8,128)(2,1)S(1)}, bf16[256,128]{0,1:T(8,128)(2,1)S(1)}, u32[]{:S(2)}, u32[]{:S(2)}) collective-permute-start(bf16[256,128]{0,1:T(8,128)(2,1)S(1)} %bitcast.67), channel_id=1, source_target_pairs={{0,20},{4,24},{8,28},{12,32},{16,36},{20,40},{24,44},{28,48},{32,5... | collective-permute-start | bytes 196616 | tf_op jit(solution)/shard_map/ppermute | solution.py:18
  68.2 1.7 collective-permute-done.3
  69.9 0.8 constant_dynamic-update-slice_fusion.4
  70.8 8.0 %fusion.1 = (f32[8,256]{1,0:T(8,128)S(1)}, f32[2304,256,8]{1,0,2:T(8,128)}) fusion(pred[256,2304]{0,1:T(8,128)(4,1)S(1)} %compare_and_fusion, bf16[256,8,32]{0,2,1:T(8,128)(2,1)S(1)} %get-tuple-element.9, bf16[256,8,32]{0,2,1:T(8,128)(2,1)S(1)} %get-tuple-element.8, bf16[2304,1,2,64]{0,3,2,1:T(8,128)(2,1)S(1)} %constant_dynamic-update-slice_fusion), kind=kOutput, calls=%fused_computation.4 | convolution fusion | flops 618657792 | bytes 20029440 | tf_op jit(solution)/shard_map/qcgd,kcd->cgqk/dot_general | solution.py:90
  78.8 10.2 %fusion = f32[8,256]{1,0:T(8,128)S(1)} fusion(f32[2304,256,8]{1,0,2:T(8,128)} %get-tuple-element.15, f32[8,256]{1,0:T(8,128)S(1)} %get-tuple-element.14, pred[256,2304]{0,1:T(8,128)(4,1)} %copy-done.3), kind=kLoop, calls=%fused_computation.3 | loop fusion | flops 18872320 | bytes 19480576 | tf_op jit(solution)/shard_map/reduce_sum | solution.py:101
  89.1 9.1 %fusion.8 = bf16[64,8,256]{2,0,1:T(8,128)(2,1)S(1)} fusion(f32[8,256]{1,0:T(8,128)S(1)} %fusion, f32[8,256]{1,0:T(8,128)S(1)} %get-tuple-element.14, f32[2304,256,8]{1,0,2:T(8,128)} %get-tuple-element.15, pred[256,2304]{0,1:T(8,128)(4,1)} %copy-done.3, bf16[2304,1,2,64]{0,3,2,1:T(8,128)(2,1)} %copy-done.4), kind=kOutput, calls=%fused_computation.21 | convolution fusion | flops 627703808 | bytes 20037632 | tf_op jit(solution)/shard_map/cgqk,kcd->qcgd/dot_general | solution.py:102
  98.2 1.7 convolution_convert_fusion.1
  100.0 57.7 %all-reduce.3.cloned.1.call-done = bf16[256,2048]{1,0:T(8,128)(2,1)} async-done(((bf16[256,2048]{1,0:T(8,128)(2,1)}), bf16[256,2048]{1,0:T(8,128)(2,1)}) %all-reduce.3.cloned.1.call-update) | async-done | bytes 1048592 | tf_op jit(solution)/shard_map/psum | solution.py:107
  157.7 1.7 multiply_reduce_fusion
  159.4 3.2 %fusion.37 = f32[256,512]{1,0:T(8,128)} fusion(bf16[2048,512]{1,0:T(8,128)(2,1)} %param.17, bf16[256,2048]{1,0:T(8,128)(2,1)S(1)} %copy-done.2, bf16[256,2048]{1,0:T(8,128)(2,1)S(1)} %copy-done.1, f32[2048]{0:T(1024)S(1)} %copy-done.7, f32[256]{0:T(256)S(1)} %add_rsqrt_fusion), kind=kOutput, calls=%fused_computation.75 | convolution fusion | flops 540016640 | bytes 4727808 | tf_op jit(solution)/shard_map/dot_general | solution.py:110
  162.6 5.1 %convolution_convert_fusion = bf16[256,2048]{1,0:T(8,128)(2,1)} fusion(bf16[512,2048]{1,0:T(8,128)(2,1)} %param.19, bf16[2048,512]{1,0:T(8,128)(2,1)} %param.18, f32[256,512]{1,0:T(8,128)} %fusion.37, bf16[256,2048]{1,0:T(8,128)(2,1)} %all-reduce.3.cloned.1.call-done, bf16[256,2048]{1,0:T(8,128)(2,1)S(1)} %copy-done.1, f32[2048]{0:T(1024)S(1)} %copy-done.7, ...), kind=kOutput, calls=%fused_computation.10 | convolution fusion | flops 1078198272 | bytes 7873536 | tf_op jit(solution)/shard_map/dot_general | solution.py:114
  167.7 0.7 copy.21
  168.5 51.6 %all-reduce.5.cloned.1.call-done = bf16[256,2048]{1,0:T(8,128)(2,1)} async-done(((bf16[256,2048]{1,0:T(8,128)(2,1)}), bf16[256,2048]{1,0:T(8,128)(2,1)}) %all-reduce.5.cloned.1.call-update) | async-done | bytes 1048592 | tf_op jit(solution)/shard_map/psum | solution.py:113
  220.1 3.1 %add_convert_fusion = bf16[256,2048]{1,0:T(8,128)(2,1)} fusion(bf16[256,2048]{1,0:T(8,128)(2,1)} %all-reduce.5.cloned.1.call-done, bf16[256,2048]{1,0:T(8,128)(2,1)} %all-reduce.3.cloned.1.call-done, bf16[256,2048]{1,0:T(8,128)(2,1)S(1)} %copy-done.1), kind=kLoop, calls=%fused_computation.16 | loop fusion | flops 3145728 | bytes 4194304 | tf_op jit(solution)/shard_map/convert_element_type | solution.py:116
  (45 shorter events, 0.5 us)
Async XLA Ops:
  7.2 91.0 %copy-start = (bf16[512,2048]{1,0:T(8,128)(2,1)S(1)}, bf16[512,2048]{1,0:T(8,128)(2,1)}, u32[]{:S(2)}) copy-start(bf16[512,2048]{1,0:T(8,128)(2,1)} %param.15) | copy-start | bytes 6291460
  7.2 41.0 %copy-start.1 = (bf16[256,2048]{1,0:T(8,128)(2,1)S(1)}, bf16[256,2048]{1,0:T(8,128)(2,1)}, u32[]{:S(2)}) copy-start(bf16[256,2048]{1,0:T(8,128)(2,1)} %param.10) | copy-start | bytes 3145732
  7.2 22.7 %copy-start.5 = (s32[256]{0:T(256)S(1)}, s32[256]{0:T(256)}, u32[]{:S(2)}) copy-start(s32[256]{0:T(256)} %param.11) | copy-start | bytes 3076
  7.2 150.5 %all-reduce.3.cloned.1.call-start = ((), (), s32[]{:S(2)}) async-start(), calls=%async_computation | async-start | bytes 2097152 | tf_op jit(solution)/shard_map/psum | solution.py:107
  8.9 2.0 copy-start.6
  11.2 59.6 %collective-permute-start.7 = (bf16[256,128]{0,1:T(8,128)(2,1)S(1)}, bf16[256,128]{0,1:T(8,128)(2,1)S(1)}, u32[]{:S(2)}, u32[]{:S(2)}) collective-permute-start(bf16[256,128]{0,1:T(8,128)(2,1)S(1)} %bitcast.60), channel_id=1, source_target_pairs={{0,4},{4,8},{8,12},{12,16},{16,20},{20,24},{24,28},{28,32},{32,36}... | collective-permute-start | bytes 196616 | tf_op jit(solution)/shard_map/ppermute | solution.py:18
  13.1 57.6 %collective-permute-start.6 = (bf16[256,128]{0,1:T(8,128)(2,1)S(1)}, bf16[256,128]{0,1:T(8,128)(2,1)S(1)}, u32[]{:S(2)}, u32[]{:S(2)}) collective-permute-start(bf16[256,128]{0,1:T(8,128)(2,1)S(1)} %bitcast.61), channel_id=1, source_target_pairs={{0,8},{4,12},{8,16},{12,20},{16,24},{20,28},{24,32},{28,36},{32,40... | collective-permute-start | bytes 196616 | tf_op jit(solution)/shard_map/ppermute | solution.py:18
  16.5 54.2 %collective-permute-start.5 = (bf16[256,128]{0,1:T(8,128)(2,1)S(1)}, bf16[256,128]{0,1:T(8,128)(2,1)S(1)}, u32[]{:S(2)}, u32[]{:S(2)}) collective-permute-start(bf16[256,128]{0,1:T(8,128)(2,1)S(1)} %bitcast.62), channel_id=1, source_target_pairs={{0,12},{4,16},{8,20},{12,24},{16,28},{20,32},{24,36},{28,40},{32,4... | collective-permute-start | bytes 196616 | tf_op jit(solution)/shard_map/ppermute | solution.py:18
  20.9 49.0 %collective-permute-start.4 = (bf16[256,128]{0,1:T(8,128)(2,1)S(1)}, bf16[256,128]{0,1:T(8,128)(2,1)}, u32[]{:S(2)}, u32[]{:S(2)}) collective-permute-start(bf16[256,128]{0,1:T(8,128)(2,1)S(1)} %bitcast.63), channel_id=1, source_target_pairs={{0,16},{4,20},{8,24},{12,28},{16,32},{20,36},{24,40},{28,44},{32,4... | collective-permute-start | bytes 196616 | tf_op jit(solution)/shard_map/ppermute | solution.py:18
  25.8 26.2 %collective-permute-start = (bf16[256,128]{0,1:T(8,128)(2,1)S(1)}, bf16[256,128]{0,1:T(8,128)(2,1)}, u32[]{:S(2)}, u32[]{:S(2)}) collective-permute-start(bf16[256,128]{0,1:T(8,128)(2,1)S(1)} %bitcast.64), channel_id=1, source_target_pairs={{0,32},{4,36},{8,40},{12,44},{16,48},{20,52},{24,56},{28,60},{32,6... | collective-permute-start | bytes 196616 | tf_op jit(solution)/shard_map/ppermute | solution.py:18
  51.9 26.9 %copy-start.3 = (pred[256,2304]{0,1:T(8,128)(4,1)}, pred[256,2304]{0,1:T(8,128)(4,1)S(1)}, u32[]{:S(2)}) copy-start(pred[256,2304]{0,1:T(8,128)(4,1)S(1)} %compare_and_fusion) | copy-start | bytes 1769476
  52.1 3.2 %collective-permute-start.1 = (bf16[256,128]{0,1:T(8,128)(2,1)S(1)}, bf16[256,128]{0,1:T(8,128)(2,1)S(1)}, u32[]{:S(2)}, u32[]{:S(2)}) collective-permute-start(bf16[256,128]{0,1:T(8,128)(2,1)S(1)} %bitcast.65), channel_id=1, source_target_pairs={{0,28},{4,32},{8,36},{12,40},{16,44},{20,48},{24,52},{28,56},{32,6... | collective-permute-start | bytes 196616 | tf_op jit(solution)/shard_map/ppermute | solution.py:18
  55.2 9.4 %collective-permute-start.2 = (bf16[256,128]{0,1:T(8,128)(2,1)S(1)}, bf16[256,128]{0,1:T(8,128)(2,1)S(1)}, u32[]{:S(2)}, u32[]{:S(2)}) collective-permute-start(bf16[256,128]{0,1:T(8,128)(2,1)S(1)} %bitcast.66), channel_id=1, source_target_pairs={{0,24},{4,28},{8,32},{12,36},{16,40},{20,44},{24,48},{28,52},{32,5... | collective-permute-start | bytes 196616 | tf_op jit(solution)/shard_map/ppermute | solution.py:18
  64.6 5.3 %collective-permute-start.3 = (bf16[256,128]{0,1:T(8,128)(2,1)S(1)}, bf16[256,128]{0,1:T(8,128)(2,1)S(1)}, u32[]{:S(2)}, u32[]{:S(2)}) collective-permute-start(bf16[256,128]{0,1:T(8,128)(2,1)S(1)} %bitcast.67), channel_id=1, source_target_pairs={{0,20},{4,24},{8,28},{12,32},{16,36},{20,40},{24,44},{28,48},{32,5... | collective-permute-start | bytes 196616 | tf_op jit(solution)/shard_map/ppermute | solution.py:18
  70.8 8.0 %copy-start.4 = (bf16[2304,1,2,64]{0,3,2,1:T(8,128)(2,1)}, bf16[2304,1,2,64]{0,3,2,1:T(8,128)(2,1)S(1)}, u32[]{:S(2)}) copy-start(bf16[2304,1,2,64]{0,3,2,1:T(8,128)(2,1)S(1)} %constant_dynamic-update-slice_fusion) | copy-start | bytes 1769476
  99.9 59.5 %copy-start.7 = (f32[2048]{0:T(1024)S(1)}, f32[2048]{0:T(1024)}, u32[]{:S(2)}) copy-start(f32[2048]{0:T(1024)} %param.16) | copy-start | bytes 24580
  99.9 120.2 %all-reduce.5.cloned.1.call-start = ((), (), s32[]{:S(2)}) async-start(), calls=%async_computation.1 | async-start | bytes 2097152 | tf_op jit(solution)/shard_map/psum | solution.py:113
  157.7 1.8 copy-start.2
Sparse Core Ops, SparseCore 0:
  100.0 57.5 all-reduce.2
  167.9 52.1 all-reduce.4
where the time goes:
time: 231 us; the launch traced here: 230 us
  waiting for transfers between devices  114 us (49%)
  matrix products  31.6 us (14%)
  starting transfers between devices  30.9 us (13%)
  other arithmetic  19.2 us (8%)
  blocking collectives  17.4 us (8%)
  between operations  14.4 us (6%)
  local copies, waits for them, and re-layouts  2.52 us (1%)
    psum x1, waiting for transfers between devices, body(): lax.psum(partial_value.astype(jnp.bfloat16), 'tp').astype(jnp.float32)  57.7 us
    psum x1, waiting for transfers between devices, body(): lax.psum(jnp.dot(hidden, down_weight, preferred_element_type=jnp.float32)...  51.6 us
    ppermute x8, starting transfers between devices, passed_along(): return lax.ppermute(x, axis, pairs)  30.8 us
    pmin x1, blocking collectives, body(): firsts = lax.pmin(local_first, 'req')  17.4 us
    reduce_sum x1, other arithmetic, body(): jnp.sum(weights, axis=-1, keepdims=True)  10.2 us
    dot_general x1, matrix products, body(): jnp.einsum('cgqk,kcd->qcgd', weights, pairs[:, :, 1], preferred_element_t...  9.07 us
    dot_general x1, matrix products, body(): jnp.einsum('qcgd,kcd->cgqk', grouped, pairs[:, :, 0], preferred_element_t...  8 us
    dot_general x1, matrix products, body(): jnp.dot(hidden, down_weight, preferred_element_type=jnp.float32)  5.1 us
  transfers between devices with their start and end apart: 10, of which 5 were waited for; matrix products, arithmetic and copies ran while one was open for 3% of the time, Pallas kernels for 0%

commit v1 on v0

v1 whole, which is shorter than its diff:
```python
import math

import jax
import jax.numpy as jnp
import numpy as np
from jax import lax
from jax.experimental import pallas as pl
from jax.experimental.pallas import tpu as pltpu
from jax.sharding import PartitionSpec as P

MESH = pl.DeviceIdType.MESH
F32 = jnp.float32
BF16 = jnp.bfloat16
NEG = -1e30
EPS = 1e-05

T = 256
D = 2048
REQ = 64
TP = 4
HEADS = 8
HD = 64
C = 512
F = 512
CH = T // TP
HALF = D // 2
BLOCKS = 8
KROWS = T + 16


def rope_tables():
    freq = np.exp(-math.log(10000.0) * np.arange(32, dtype=np.float32) / np.float32(32)).astype(np.float32)
    freq = np.tile(freq.astype(np.float64), 4)[None, :]
    base = (np.arange(REQ) * T)[:, None] * freq
    inner = np.arange(T)[:, None] * freq
    base = np.stack([np.cos(base), np.sin(base)]).astype(np.float32)
    inner = np.stack([np.cos(inner), np.sin(inner)]).astype(np.float32)
    return base, inner


def iota(shape, dim):
    return lax.broadcasted_iota(jnp.int32, shape, dim)


def kernel(
    tok_h, seg_ref, g1_ref, g2_ref, base_ref, inner_ref,
    qw_h, pw_h, ow_h, gw_h, uw_h, dw_h,
    out_h, kvout_h,
    tok, normed, pw, qw, ow, gw, uw, dw,
    kvb, kT, vx, qa, S, M, Pm, ho, hid, sb, rb, own, own2, res, mid, outb,
    ld, kvo, oo, dsend, drecv, fsend, frecv, rsend, rrecv, asend, arecv,
):
    r = lax.axis_index("req")
    y = lax.axis_index("tp")
    core = lax.rem(r, 2)
    partner = r + 1 - 2 * core
    right = lax.rem(y + 1, TP)
    left = lax.rem(y + 3, TP)
    opp = lax.rem(y + 2, TP)

    barrier = pltpu.get_barrier_semaphore()
    for k in range(1, 5):
        pl.semaphore_signal(
            barrier, inc=1, device_id=(lax.rem(r + REQ - 2 * k, REQ), y), device_id_type=MESH
        )
    pl.semaphore_signal(barrier, inc=1, device_id=(partner, y), device_id_type=MESH)
    pl.semaphore_signal(barrier, inc=1, device_id=(r, right), device_id_type=MESH)
    pl.semaphore_signal(barrier, inc=1, device_id=(r, left), device_id_type=MESH)

    def load(i, src, dst):
        return pltpu.make_async_copy(src, dst, ld.at[i])

    loads = [
        load(i, s, d)
        for i, (s, d) in enumerate(
            [(tok_h, tok), (pw_h, pw), (qw_h, qw), (ow_h, ow), (gw_h, gw), (uw_h, uw), (dw_h, dw)]
        )
    ]
    for c in loads[:3]:
        c.start()

    ca, sa = base_ref[0, pl.ds(r, 1), :], base_ref[1, pl.ds(r, 1), :]
    cb, sn = inner_ref[0], inner_ref[1]
    cos = ca * cb - sa * sn
    sin = sa * cb + ca * sn
    lane = iota((T, 128), 1)
    first = lax.rem(lane, 64) < 32
    s_up = jnp.where(first, -sin, 0.0)
    s_dn = jnp.where(first, 0.0, sin)

    def rotate(x, c, su, sd):
        return x * c + pltpu.roll(x, 96, 1) * su + pltpu.roll(x, 32, 1) * sd

    seg_row = seg_ref[...].astype(F32)
    seg_col = jnp.broadcast_to(seg_row, (128, T)).T
    loads[0].wait()

    def norm_rows(i, carry):
        rows = pl.ds(pl.multiple_of(i * 16, 16), 16)
        x = tok[rows, :].astype(F32)
        ms = jnp.mean(x * x, axis=-1, keepdims=True)
        normed[rows, :] = (x * lax.rsqrt(ms + EPS) * g1_ref[...]).astype(BF16)
        return carry

    lax.fori_loop(0, T // 16, norm_rows, 0, unroll=2)

    loads[1].wait()
    kv = jnp.dot(normed[...], pw[...], preferred_element_type=F32)
    isk = lane < 64
    kv = rotate(kv, jnp.where(isk, cos, 1.0), jnp.where(isk, s_up, 0.0), jnp.where(isk, s_dn, 0.0))
    kvb[0, 0:T, :] = kv.astype(BF16)
    srow = iota((16, 128), 0)
    kvb[0, T:KROWS, :] = jnp.where(
        srow == 0, seg_row[:, :128], jnp.where(srow == 1, seg_row[:, 128:], 0.0)
    ).astype(BF16)

    pl.semaphore_wait(barrier, 7)

    def direct(k):
        return pltpu.make_async_remote_copy(
            src_ref=kvb.at[0], dst_ref=kvb.at[2 * k],
            send_sem=dsend.at[k - 1], recv_sem=drecv.at[k - 1],
            device_id=(lax.rem(r + 2 * k, REQ), y), device_id_type=MESH,
        )

    def forward(j, src):
        return pltpu.make_async_remote_copy(
            src_ref=kvb.at[src], dst_ref=kvb.at[2 * j + 1],
            send_sem=fsend.at[j], recv_sem=frecv.at[j],
            device_id=(partner, y), device_id_type=MESH,
        )

    for k in (4, 3, 2, 1):
        direct(k).start()

    @pl.when(core == 0)
    def _():
        forward(0, 0).start()

    kv_copy = pltpu.make_async_copy(kvb.at[0, 0:T, :], kvout_h, kvo)
    kv_copy.start()
    for c in loads[3:]:
        c.start()

    loads[2].wait()
    qpen = jnp.where((lane - 64).astype(F32) == seg_col, NEG, 0.0)
    qpen = jnp.where(lane < 80, qpen, 0.0)
    for n in range(2):
        q4 = jnp.dot(normed[...], qw[:, n * 256:(n + 1) * 256], preferred_element_type=F32)
        for i in range(2):
            q2 = rotate(q4[:, i * 128:(i + 1) * 128], cos, s_up, s_dn) * (HD ** -0.5)
            h = n * 4 + i * 2
            qa[h] = jnp.where(isk, q2, qpen).astype(BF16)
            qa[h + 1] = jnp.where(isk, pltpu.roll(q2, 64, 1), qpen).astype(BF16)

    def prepare(d):
        kv = kvb[d, 0:T, :].astype(F32)
        ids = kvb[d, T:KROWS, :].astype(F32)
        ids = jnp.concatenate([ids[0:1], ids[1:2]], axis=1) + jnp.where(r >= d, 0.0, 100.0)
        row = iota((128, T), 0)
        differs = jnp.where((row - 64).astype(F32) == ids, 0.0, 1.0)
        kT[d] = jnp.where(row < 64, kv.T, jnp.where(row < 80, differs, 0.0)).astype(BF16)
        vx[d * T:(d + 1) * T, :] = jnp.where(isk, pltpu.roll(kv, 64, 1), 1.0).astype(BF16)

    def score(d):
        def body(h, carry):
            s = jnp.dot(qa[h], kT[d], preferred_element_type=F32)
            at = (d % BLOCKS) * T
            if d in (0, BLOCKS):
                seen = iota((T, T), 1) <= iota((T, T), 0)
                s = jnp.where(seen, s if d == 0 else S[h, :, 0:T], NEG if d == 0 else s)
            S[h, :, at:at + T] = s
            top = jnp.maximum(s[:, :128], s[:, 128:])
            M[h] = top if d == 0 else jnp.maximum(M[h], top)
            return carry

        lax.fori_loop(0, HEADS, body, 0)

    prepare(0)
    score(0)
    for k in range(1, 5):
        direct(k).wait_recv()

        @pl.when(core == 1)
        def _():
            forward(k - 1, 2 * k).start()

        if k < 4:
            @pl.when(core == 0)
            def _():
                forward(k, 2 * k).start()

        prepare(2 * k)
        score(2 * k)
        forward(k - 1, 0).wait_recv()
        prepare(2 * k - 1)
        score(2 * k - 1)

    loads[3].wait()

    def attend(chunk):
        r0 = pl.multiple_of(chunk * CH, CH)
        rows = pl.ds(r0, CH)

        def head(h, carry):
            m = jnp.max(M[h, rows, :], axis=1, keepdims=True)
            to = pl.ds(pl.multiple_of(h * CH, CH), CH)
            for b in range(BLOCKS):
                p = jnp.exp(S[h, rows, b * T:(b + 1) * T] - m)
                if b == 0:
                    seen = iota((CH, T), 1) <= iota((CH, T), 0) + r0
                    Pm[to, BLOCKS * T:(BLOCKS + 1) * T] = jnp.where(seen, 0.0, p).astype(BF16)
                    p = jnp.where(seen, p, 0.0)
                Pm[to, b * T:(b + 1) * T] = p.astype(BF16)
            return carry

        lax.fori_loop(0, HEADS, head, 0)
        low = iota((CH, 128), 1) < 64
        for n in range(2):
            o = jnp.dot(Pm[n * 256:(n + 1) * 256, :], vx[...], preferred_element_type=F32)
            o = o / pltpu.roll(o, 64, 1)
            for i in range(2):
                even, odd = o[i * 128:i * 128 + 64], o[i * 128 + 64:i * 128 + 128]
                at = (n * 2 + i) * 128
                ho[:, at:at + 128] = jnp.where(low, even, pltpu.roll(odd, 64, 1)).astype(BF16)

    def project(x, w, n):
        return jnp.dot(x[...], w[:, n * HALF:(n + 1) * HALF], preferred_element_type=F32).astype(BF16)

    def rs(round_, i):
        at = round_ * 6 + i
        return pltpu.make_async_remote_copy(
            src_ref=sb.at[at], dst_ref=rb.at[at], send_sem=rsend.at[at], recv_sem=rrecv.at[at],
            device_id=(r, right if i < 3 else left), device_id_type=MESH,
        )

    attend(opp)
    sb[0] = project(ho, ow, 0)
    rs(0, 0).start()
    sb[3] = project(ho, ow, 1)
    rs(0, 3).start()
    attend(right)
    sb[2] = project(ho, ow, 1)
    rs(0, 2).start()
    part = project(ho, ow, 0)
    rs(0, 0).wait_recv()
    sb[1] = (part.astype(F32) + rb[0].astype(F32)).astype(BF16)
    rs(0, 1).start()
    attend(left)
    sb[5] = project(ho, ow, 0)
    rs(0, 5).start()
    part = project(ho, ow, 1)
    rs(0, 3).wait_recv()
    sb[4] = (part.astype(F32) + rb[3].astype(F32)).astype(BF16)
    rs(0, 4).start()
    attend(y)
    for n in range(2):
        own[:, n * HALF:(n + 1) * HALF] = project(ho, ow, n)

    mine = pl.ds(pl.multiple_of(y * CH, CH), CH)
    for i in (1, 2, 4, 5):
        rs(0, i).wait_recv()

    def mix(i, carry):
        at = pl.multiple_of(i * 16, 16)
        rows = pl.ds(at, 16)
        x = tok[pl.ds(pl.multiple_of(y * CH + i * 16, 16), 16), :].astype(F32)
        o = own[rows, :].astype(F32)
        add_a = rb[1, rows, :].astype(F32) + rb[5, rows, :].astype(F32)
        add_b = rb[2, rows, :].astype(F32) + rb[4, rows, :].astype(F32)
        x = x + o + jnp.concatenate([add_a, add_b], axis=1)
        res[rows, :] = x
        ms = jnp.mean(x * x, axis=-1, keepdims=True)
        mid[pl.ds(pl.multiple_of(y * CH + i * 16, 16), 16), :] = (
            x * lax.rsqrt(ms + EPS) * g2_ref[...]
        ).astype(BF16)
        return carry

    lax.fori_loop(0, CH // 16, mix, 0)

    def ag(round_, i, buf):
        at = round_ * 6 + i
        chunk = (y, y, left, y, y, right)[i]
        half = (0, 1, 0, 1, 0, 1)[i]
        where = buf.at[pl.ds(pl.multiple_of(chunk * CH, CH), CH), pl.ds(half * HALF, HALF)]
        return pltpu.make_async_remote_copy(
            src_ref=where, dst_ref=where, send_sem=asend.at[at], recv_sem=arecv.at[at],
            device_id=(r, right if i < 3 else left), device_id_type=MESH,
        )

    def gather_start(round_, buf):
        for i in (0, 3, 1, 4):
            ag(round_, i, buf).start()

    def gather_pass(round_, buf):
        ag(round_, 0, buf).wait_recv()
        ag(round_, 2, buf).start()
        ag(round_, 3, buf).wait_recv()
        ag(round_, 5, buf).start()

    gather_start(0, mid)
    for c in loads[4:]:
        c.wait()

    def feed(chunk):
        x = mid[pl.ds(pl.multiple_of(chunk * CH, CH), CH), :]
        for n in range(2):
            cols = slice(n * 256, (n + 1) * 256)
            g = jnp.dot(x, gw[:, cols], preferred_element_type=F32)
            u = jnp.dot(x, uw[:, cols], preferred_element_type=F32)
            hid[:, cols] = (g / (1.0 + jnp.exp(-g)) * u).astype(BF16)

    feed(y)
    for n in range(2):
        own2[:, n * HALF:(n + 1) * HALF] = project(hid, dw, n)
    gather_pass(0, mid)
    ag(0, 1, mid).wait_recv()
    feed(left)
    sb[11] = project(hid, dw, 0)
    rs(1, 5).start()
    sb[10] = project(hid, dw, 1)
    ag(0, 4, mid).wait_recv()
    feed(right)
    sb[8] = project(hid, dw, 1)
    rs(1, 2).start()
    sb[7] = project(hid, dw, 0)
    ag(0, 2, mid).wait_recv()
    ag(0, 5, mid).wait_recv()
    feed(opp)
    sb[6] = project(hid, dw, 0)
    rs(1, 0).start()
    sb[9] = project(hid, dw, 1)
    rs(1, 3).start()
    rs(1, 0).wait_recv()
    sb[7] = (sb[7].astype(F32) + rb[6].astype(F32)).astype(BF16)
    rs(1, 1).start()
    rs(1, 3).wait_recv()
    sb[10] = (sb[10].astype(F32) + rb[9].astype(F32)).astype(BF16)
    rs(1, 4).start()
    for i in (1, 2, 4, 5):
        rs(1, i).wait_recv()

    def finish(i, carry):
        rows = pl.ds(pl.multiple_of(i * 16, 16), 16)
        o = own2[rows, :].astype(F32)
        add_a = rb[7, rows, :].astype(F32) + rb[11, rows, :].astype(F32)
        add_b = rb[8, rows, :].astype(F32) + rb[10, rows, :].astype(F32)
        x = res[rows, :] + (o + jnp.concatenate([add_a, add_b], axis=1))
        outb[pl.ds(pl.multiple_of(y * CH + i * 16, 16), 16), :] = x.astype(BF16)
        return carry

    lax.fori_loop(0, CH // 16, finish, 0)
    gather_start(1, outb)

    def put(i, chunk):
        rows = pl.ds(pl.multiple_of(chunk * CH, CH), CH)
        return pltpu.make_async_copy(outb.at[rows, :], out_h.at[rows, :], oo.at[i])

    put(0, y).start()
    gather_pass(1, outb)
    ag(1, 1, outb).wait_recv()
    put(1, left).start()
    ag(1, 4, outb).wait_recv()
    put(2, right).start()
    ag(1, 2, outb).wait_recv()
    ag(1, 5, outb).wait_recv()
    put(3, opp).start()

    for k in range(1, 5):
        direct(k).wait_send()
        forward(k - 1, 0).wait_send()
    for i in range(6):
        rs(0, i).wait_send()
        rs(1, i).wait_send()
        ag(0, i, mid).wait_send()
        ag(1, i, outb).wait_send()
    kv_copy.wait()
    for i, chunk in enumerate((y, left, right, opp)):
        put(i, chunk).wait()


def body(tokens, segment_ids, mixer_gain, query_weight, pair_weight, output_weight, feed_gain,
         gate_weight, up_weight, down_weight):
    base, inner = rope_tables()
    hbm = pl.BlockSpec(memory_space=pl.ANY)
    vm = pl.BlockSpec(memory_space=pltpu.VMEM)
    dma = pltpu.SemaphoreType.DMA
    return pl.pallas_call(
        kernel,
        out_shape=(
            jax.ShapeDtypeStruct((T, D), BF16),
            jax.ShapeDtypeStruct((T, 128), BF16),
        ),
        in_specs=[hbm, vm, vm, vm, vm, vm] + [hbm] * 6,
        out_specs=(hbm, hbm),
        scratch_shapes=[
            pltpu.VMEM((T, D), BF16),
            pltpu.VMEM((T, D), BF16),
            pltpu.VMEM((D, 128), BF16),
            pltpu.VMEM((D, C), BF16),
            pltpu.VMEM((C, D), BF16),
            pltpu.VMEM((D, F), BF16),
            pltpu.VMEM((D, F), BF16),
            pltpu.VMEM((F, D), BF16),
            pltpu.VMEM((BLOCKS + 1, KROWS, 128), BF16),
            pltpu.VMEM((BLOCKS + 1, 128, T), BF16),
            pltpu.VMEM(((BLOCKS + 1) * T, 128), BF16),
            pltpu.VMEM((HEADS, T, 128), BF16),
            pltpu.VMEM((HEADS, T, BLOCKS * T), F32),
            pltpu.VMEM((HEADS, T, 128), F32),
            pltpu.VMEM((HEADS * CH, (BLOCKS + 1) * T), BF16),
            pltpu.VMEM((CH, C), BF16),
            pltpu.VMEM((CH, F), BF16),
            pltpu.VMEM((12, CH, HALF), BF16),
            pltpu.VMEM((12, CH, HALF), BF16),
            pltpu.VMEM((CH, D), BF16),
            pltpu.VMEM((CH, D), BF16),
            pltpu.VMEM((CH, D), F32),
            pltpu.VMEM((T, D), BF16),
            pltpu.VMEM((T, D), BF16),
            dma((7,)), dma, dma((4,)),
            dma((4,)), dma((4,)), dma((4,)), dma((4,)),
            dma((12,)), dma((12,)), dma((12,)), dma((12,)),
        ],
        compiler_params=pltpu.CompilerParams(
            collective_id=0, has_side_effects=True, vmem_limit_bytes=64 * 1024 * 1024 - 65536
        ),
        name="block",
    )(
        tokens, segment_ids.reshape(1, T), mixer_gain.reshape(1, D), feed_gain.reshape(1, D),
        jnp.asarray(base), jnp.asarray(inner),
        query_weight, pair_weight, output_weight, gate_weight, up_weight, down_weight,
    )


def solution(mesh):
    return jax.shard_map(
        body,
        mesh=mesh,
        in_specs=(
            P("req", None),
            P("req"),
            P(),
            P(None, "tp"),
            P(None, "tp"),
            P("tp", None),
            P(),
            P(None, "tp"),
            P(None, "tp"),
            P("tp", None),
        ),
        out_specs=(P("req", None), P("req", "tp")),
        check_vma=False,
    )
```

time: 231 us -> 83.3 us (0.36)
  waiting for transfers between devices: 114 us -> 0 us
  Pallas kernels: 0 us -> 79.2 us
  matrix products: 31.6 us -> 0 us
  starting transfers between devices: 30.9 us -> 0 us
  other arithmetic: 19.2 us -> 0 us
  blocking collectives: 17.4 us -> 0 us
  between operations: 14.4 us -> 0.65 us
    psum x2 -> x0, waiting for transfers between devices: 109 us -> none  [the longest x1 57.7 us: body(): lax.psum(partial_value.astype(jnp.bfloat16), 'tp').astype(jnp.float32)]
    pallas_call x0 -> x1, Pallas kernels: none -> 79.2 us  [body(): pl.pallas_call(kernel, out_shape=(jax.ShapeDtypeStruct((T, D), BF16), jax...]
    dot_general x7 -> x0, matrix products: 31.6 us -> none  [the longest x1 9.07 us: body(): jnp.einsum('cgqk,kcd->qcgd', weights, pairs[:, :, 1], preferred_element_t...]
    ppermute x8 -> x0, starting transfers between devices: 30.8 us -> none  [passed_along(): return lax.ppermute(x, axis, pairs)]
    pmin x1 -> x0, blocking collectives: 17.4 us -> none  [body(): firsts = lax.pmin(local_first, 'req')]
    reduce_sum x4 -> x0, other arithmetic: 14.4 us -> none  [the longest x1 10.2 us: body(): jnp.sum(weights, axis=-1, keepdims=True)]
    ppermute x8 -> x0, waiting for transfers between devices: 4.61 us -> none  [passed_along(): return lax.ppermute(x, axis, pairs)]
    convert_element_type x3 -> x0, other arithmetic: 3.11 us -> none  [the longest x1 3.09 us: body(): block_output = (residual + feed_out).astype(jnp.bfloat16)]
  transfers between devices with their start and end apart: 10 -> 0, of which waited for: 5 -> 0; matrix products, arithmetic and copies ran while one was open for 3% -> 0% of each run, Pallas kernels for 0% -> 0%
where the time goes in v1:
time: 83.3 us; the launch traced here: 82.8 us
  Pallas kernels  79.2 us (95%)
  local copies, waits for them, and re-layouts  2.97 us (4%)
    pallas_call x1, Pallas kernels, body(): pl.pallas_call(kernel, out_shape=(jax.ShapeDtypeStruct((T, D), BF16), jax...  79.2 us
    unnamed x4, local copies, waits for them, and re-layouts  2.97 us

profile of v1, /device:TPU:2, one launch (start us, length us, event | category | flops | bytes accessed | tf_op | source)
XLA Modules:
  0.0 82.8 jit_solution(11002322859922855313)
XLA Ops:
  0.6 79.2 %block.1 = (bf16[256,2048]{1,0:T(8,128)(2,1)}, bf16[256,128]{1,0:T(8,128)(2,1)}) custom-call(bf16[256,2048]{1,0:T(8,128)(2,1)} %tok_h.1, s32[1,256]{1,0:T(1,128)} %bitcast.5, f32[1,2048]{1,0:T(1,128)} %bitcast.3, f32[1,2048]{1,0:T(1,128)} %bitcast.4, f32[2,64,128]{2,1,0:T(8,128)} %constant.4.clone.base_ref, f32[2,256,128]{2,1,0:T(8,128)} %constant.5.clone.inner_ref, ...), custom_call_target="tpu_custom_call" | custom-call | tf_op jit(solution)/shard_map/block/pallas_call | solution.py:388
  79.8 0.0 copy-start
  79.8 2.3 %copy.16 = bf16[256,2048]{1,0:T(8,128)(2,1)} copy(bf16[256,2048]{1,0:T(8,128)(2,1)} %get-tuple-element.4) | data formatting | bytes 2097152
  82.2 0.0 copy-done
  82.2 0.6 copy.17
Async XLA Ops:
  79.8 2.3 %copy-start = (bf16[256,128]{1,0:T(8,128)(2,1)S(1)}, bf16[256,128]{1,0:T(8,128)(2,1)}, u32[]{:S(2)}) copy-start(bf16[256,128]{1,0:T(8,128)(2,1)} %get-tuple-element.5) | copy-start | bytes 196612

commit v2 on v1

--- a/solution.py
+++ b/solution.py
@@ -47,7 +47,7 @@
     qw_h, pw_h, ow_h, gw_h, uw_h, dw_h,
     out_h, kvout_h,
     tok, normed, pw, qw, ow, gw, uw, dw,
-    kvb, kT, vx, qa, S, M, Pm, ho, hid, sb, rb, own, own2, res, mid, outb,
+    kvb, kT, vx, qa, S, M, Pm, ho, sb, rb, own, own2, res, mid, outb,
     ld, kvo, oo, dsend, drecv, fsend, frecv, rsend, rrecv, asend, arecv,
 ):
     r = lax.axis_index("req")
@@ -130,7 +130,7 @@
             device_id=(partner, y), device_id_type=MESH,
         )
 
-    for k in (4, 3, 2, 1):
+    for k in range(1, 5):
         direct(k).start()
 
     @pl.when(core == 0)
@@ -162,7 +162,9 @@
         kT[d] = jnp.where(row < 64, kv.T, jnp.where(row < 80, differs, 0.0)).astype(BF16)
         vx[d * T:(d + 1) * T, :] = jnp.where(isk, pltpu.roll(kv, 64, 1), 1.0).astype(BF16)
 
-    def score(d):
+    def top(d):
+        prepare(d)
+
         def body(h, carry):
             s = jnp.dot(qa[h], kT[d], preferred_element_type=F32)
             at = (d % BLOCKS) * T
@@ -176,9 +178,7 @@
 
         lax.fori_loop(0, HEADS, body, 0)
 
-    prepare(0)
-    score(0)
-    for k in range(1, 5):
+    def arrive(k):
         direct(k).wait_recv()
 
         @pl.when(core == 1)
@@ -190,11 +190,16 @@
             def _():
                 forward(k, 2 * k).start()
 
-        prepare(2 * k)
-        score(2 * k)
-        forward(k - 1, 0).wait_recv()
-        prepare(2 * k - 1)
-        score(2 * k - 1)
+    top(0)
+    arrive(1)
+    top(2)
+    for k in range(2, 5):
+        arrive(k)
+        forward(k - 2, 0).wait_recv()
+        top(2 * k - 3)
+        top(2 * k)
+    forward(3, 0).wait_recv()
+    top(7)
 
     loads[3].wait()
 
@@ -302,34 +307,39 @@
     for c in loads[4:]:
         c.wait()
 
-    def feed(chunk):
-        x = mid[pl.ds(pl.multiple_of(chunk * CH, CH), CH), :]
+    def chunk_rows(chunk):
+        return mid[pl.ds(pl.multiple_of(chunk * CH, CH), CH), :]
+
+    def feed(x):
+        hs = []
         for n in range(2):
             cols = slice(n * 256, (n + 1) * 256)
             g = jnp.dot(x, gw[:, cols], preferred_element_type=F32)
             u = jnp.dot(x, uw[:, cols], preferred_element_type=F32)
-            hid[:, cols] = (g / (1.0 + jnp.exp(-g)) * u).astype(BF16)
-
-    feed(y)
+            hs.append((g / (1.0 + jnp.exp(-g)) * u).astype(BF16))
+        return jnp.concatenate(hs, axis=1)
+
+    h = feed(chunk_rows(y))
     for n in range(2):
-        own2[:, n * HALF:(n + 1) * HALF] = project(hid, dw, n)
+        own2[:, n * HALF:(n + 1) * HALF] = project(h, dw, n)
     gather_pass(0, mid)
     ag(0, 1, mid).wait_recv()
-    feed(left)
-    sb[11] = project(hid, dw, 0)
+    ag(0, 4, mid).wait_recv()
+    h = feed(jnp.concatenate([chunk_rows(left), chunk_rows(right)], axis=0))
+    part = project(h, dw, 0)
+    sb[11] = part[:CH]
     rs(1, 5).start()
-    sb[10] = project(hid, dw, 1)
-    ag(0, 4, mid).wait_recv()
-    feed(right)
-    sb[8] = project(hid, dw, 1)
+    sb[7] = part[CH:]
+    part = project(h, dw, 1)
+    sb[10] = part[:CH]
+    sb[8] = part[CH:]
     rs(1, 2).start()
-    sb[7] = project(hid, dw, 0)
     ag(0, 2, mid).wait_recv()
     ag(0, 5, mid).wait_recv()
-    feed(opp)
-    sb[6] = project(hid, dw, 0)
+    h = feed(chunk_rows(opp))
+    sb[6] = project(h, dw, 0)
     rs(1, 0).start()
-    sb[9] = project(hid, dw, 1)
+    sb[9] = project(h, dw, 1)
     rs(1, 3).start()
     rs(1, 0).wait_recv()
     sb[7] = (sb[7].astype(F32) + rb[6].astype(F32)).astype(BF16)
@@ -410,7 +420,6 @@
             pltpu.VMEM((HEADS, T, 128), F32),
             pltpu.VMEM((HEADS * CH, (BLOCKS + 1) * T), BF16),
             pltpu.VMEM((CH, C), BF16),
-            pltpu.VMEM((CH, F), BF16),
             pltpu.VMEM((12, CH, HALF), BF16),
             pltpu.VMEM((12, CH, HALF), BF16),
             pltpu.VMEM((CH, D), BF16),

time: 83.3 us -> 83.3 us (level)
  no operation moved by 1% of the time
where the time goes in v2:
time: 83.3 us; the launch traced here: 83.2 us
  Pallas kernels  79.5 us (95%)
  local copies, waits for them, and re-layouts  2.97 us (4%)
    pallas_call x1, Pallas kernels, body(): pl.pallas_call(kernel, out_shape=(jax.ShapeDtypeStruct((T, D), BF16), jax...  79.5 us
    unnamed x4, local copies, waits for them, and re-layouts  2.97 us

profile of v2, /device:TPU:2, one launch (start us, length us, event | category | flops | bytes accessed | tf_op | source)
XLA Modules:
  0.0 83.2 jit_solution(11141859051149803846)
XLA Ops:
  0.6 79.5 %block.1 = (bf16[256,2048]{1,0:T(8,128)(2,1)}, bf16[256,128]{1,0:T(8,128)(2,1)}) custom-call(bf16[256,2048]{1,0:T(8,128)(2,1)} %tok_h.1, s32[1,256]{1,0:T(1,128)} %bitcast.5, f32[1,2048]{1,0:T(1,128)} %bitcast.3, f32[1,2048]{1,0:T(1,128)} %bitcast.4, f32[2,64,128]{2,1,0:T(8,128)} %constant.4.clone.base_ref, f32[2,256,128]{2,1,0:T(8,128)} %constant.5.clone.inner_ref, ...), custom_call_target="tpu_custom_call" | custom-call | tf_op jit(solution)/shard_map/block/pallas_call | solution.py:398
  80.2 0.0 copy-start
  80.2 2.3 %copy.16 = bf16[256,2048]{1,0:T(8,128)(2,1)} copy(bf16[256,2048]{1,0:T(8,128)(2,1)} %get-tuple-element.4) | data formatting | bytes 2097152
  82.5 0.0 copy-done
  82.5 0.6 copy.17
Async XLA Ops:
  80.2 2.3 %copy-start = (bf16[256,128]{1,0:T(8,128)(2,1)S(1)}, bf16[256,128]{1,0:T(8,128)(2,1)}, u32[]{:S(2)}) copy-start(bf16[256,128]{1,0:T(8,128)(2,1)} %get-tuple-element.5) | copy-start | bytes 196612

commit v3 on v2

--- a/solution.py
+++ b/solution.py
@@ -60,9 +60,10 @@
 
     barrier = pltpu.get_barrier_semaphore()
     for k in range(1, 5):
-        pl.semaphore_signal(
-            barrier, inc=1, device_id=(lax.rem(r + REQ - 2 * k, REQ), y), device_id_type=MESH
-        )
+        @pl.when(r >= 2 * k)
+        def _():
+            pl.semaphore_signal(barrier, inc=1, device_id=(r - 2 * k, y), device_id_type=MESH)
+
     pl.semaphore_signal(barrier, inc=1, device_id=(partner, y), device_id_type=MESH)
     pl.semaphore_signal(barrier, inc=1, device_id=(r, right), device_id_type=MESH)
     pl.semaphore_signal(barrier, inc=1, device_id=(r, left), device_id_type=MESH)
@@ -76,7 +77,7 @@
             [(tok_h, tok), (pw_h, pw), (qw_h, qw), (ow_h, ow), (gw_h, gw), (uw_h, uw), (dw_h, dw)]
         )
     ]
-    for c in loads[:3]:
+    for c in loads:
         c.start()
 
     ca, sa = base_ref[0, pl.ds(r, 1), :], base_ref[1, pl.ds(r, 1), :]
@@ -114,13 +115,13 @@
         srow == 0, seg_row[:, :128], jnp.where(srow == 1, seg_row[:, 128:], 0.0)
     ).astype(BF16)
 
-    pl.semaphore_wait(barrier, 7)
+    pl.semaphore_wait(barrier, 3 + jnp.minimum(4, (REQ - 1 - r) // 2))
 
     def direct(k):
         return pltpu.make_async_remote_copy(
             src_ref=kvb.at[0], dst_ref=kvb.at[2 * k],
             send_sem=dsend.at[k - 1], recv_sem=drecv.at[k - 1],
-            device_id=(lax.rem(r + 2 * k, REQ), y), device_id_type=MESH,
+            device_id=(r + 2 * k, y), device_id_type=MESH,
         )
 
     def forward(j, src):
@@ -131,7 +132,15 @@
         )
 
     for k in range(1, 5):
-        direct(k).start()
+        @pl.when(r + 2 * k < REQ)
+        def _():
+            direct(k).start()
+
+    for d in range(1, BLOCKS + 1):
+        @pl.when(r < d)
+        def _():
+            kvb[d] = jnp.zeros((KROWS, 128), BF16)
+
 
     @pl.when(core == 0)
     def _():
@@ -139,8 +148,6 @@
 
     kv_copy = pltpu.make_async_copy(kvb.at[0, 0:T, :], kvout_h, kvo)
     kv_copy.start()
-    for c in loads[3:]:
-        c.start()
 
     loads[2].wait()
     qpen = jnp.where((lane - 64).astype(F32) == seg_col, NEG, 0.0)
@@ -179,26 +186,33 @@
         lax.fori_loop(0, HEADS, body, 0)
 
     def arrive(k):
-        direct(k).wait_recv()
-
-        @pl.when(core == 1)
+        @pl.when(r >= 2 * k)
+        def _():
+            direct(k).wait_recv()
+
+        @pl.when((r >= 2 * k) & (core == 1))
         def _():
             forward(k - 1, 2 * k).start()
 
         if k < 4:
-            @pl.when(core == 0)
+            @pl.when((r >= 2 * k) & (core == 0))
             def _():
                 forward(k, 2 * k).start()
+
+    def handed(j):
+        @pl.when(r >= 2 * j + 1)
+        def _():
+            forward(j, 0).wait_recv()
 
     top(0)
     arrive(1)
     top(2)
     for k in range(2, 5):
         arrive(k)
-        forward(k - 2, 0).wait_recv()
+        handed(k - 2)
         top(2 * k - 3)
         top(2 * k)
-    forward(3, 0).wait_recv()
+    handed(3)
     top(7)
 
     loads[3].wait()
@@ -377,8 +391,14 @@
     put(3, opp).start()
 
     for k in range(1, 5):
-        direct(k).wait_send()
-        forward(k - 1, 0).wait_send()
+        @pl.when(r + 2 * k < REQ)
+        def _():
+            direct(k).wait_send()
+
+        @pl.when(r >= 2 * (k - 1) + 2 * core)
+        def _():
+            forward(k - 1, 0).wait_send()
+
     for i in range(6):
         rs(0, i).wait_send()
         rs(1, i).wait_send()

time: 83.3 us -> 79.9 us (0.959)
  the two profiles are of different devices: /device:TPU:2 before, /device:TPU:160 now
where the time goes in v3:
time: 79.9 us; the launch traced here: 79.8 us
  Pallas kernels  76.2 us (95%)
  local copies, waits for them, and re-layouts  2.97 us (4%)
    pallas_call x1, Pallas kernels, body(): pl.pallas_call(kernel, out_shape=(jax.ShapeDtypeStruct((T, D), BF16), jax...  76.2 us
    unnamed x4, local copies, waits for them, and re-layouts  2.97 us

profile of v3, /device:TPU:160, one launch (start us, length us, event | category | flops | bytes accessed | tf_op | source)
XLA Modules:
  0.0 79.8 jit_solution(17137971345661938423)
XLA Ops:
  0.6 76.2 %block.1 = (bf16[256,2048]{1,0:T(8,128)(2,1)}, bf16[256,128]{1,0:T(8,128)(2,1)}) custom-call(bf16[256,2048]{1,0:T(8,128)(2,1)} %tok_h.1, s32[1,256]{1,0:T(1,128)} %bitcast.5, f32[1,2048]{1,0:T(1,128)} %bitcast.3, f32[1,2048]{1,0:T(1,128)} %bitcast.4, f32[2,64,128]{2,1,0:T(8,128)} %constant.4.clone.base_ref, f32[2,256,128]{2,1,0:T(8,128)} %constant.5.clone.inner_ref, ...), custom_call_target="tpu_custom_call" | custom-call | tf_op jit(solution)/shard_map/block/pallas_call | solution.py:418
  76.8 0.0 copy-start
  76.8 2.3 %copy.16 = bf16[256,2048]{1,0:T(8,128)(2,1)} copy(bf16[256,2048]{1,0:T(8,128)(2,1)} %get-tuple-element.4) | data formatting | bytes 2097152
  79.2 0.0 copy-done
  79.2 0.6 copy.17
Async XLA Ops:
  76.8 2.3 %copy-start = (bf16[256,128]{1,0:T(8,128)(2,1)S(1)}, bf16[256,128]{1,0:T(8,128)(2,1)}, u32[]{:S(2)}) copy-start(bf16[256,128]{1,0:T(8,128)(2,1)} %get-tuple-element.5) | copy-start | bytes 196612

commit v4 on v3

--- a/solution.py
+++ b/solution.py
@@ -167,20 +167,26 @@
         row = iota((128, T), 0)
         differs = jnp.where((row - 64).astype(F32) == ids, 0.0, 1.0)
         kT[d] = jnp.where(row < 64, kv.T, jnp.where(row < 80, differs, 0.0)).astype(BF16)
-        vx[d * T:(d + 1) * T, :] = jnp.where(isk, pltpu.roll(kv, 64, 1), 1.0).astype(BF16)
-
-    def top(d):
-        prepare(d)
+        v1 = jnp.where(isk, pltpu.roll(kv, 64, 1), 1.0).astype(BF16)
+        vx[d * T:(d + 1) * T, :128] = v1
+        vx[d * T:(d + 1) * T, 128:] = v1
+
+    def top(*ds):
+        for d in ds:
+            prepare(d)
 
         def body(h, carry):
-            s = jnp.dot(qa[h], kT[d], preferred_element_type=F32)
-            at = (d % BLOCKS) * T
-            if d in (0, BLOCKS):
-                seen = iota((T, T), 1) <= iota((T, T), 0)
-                s = jnp.where(seen, s if d == 0 else S[h, :, 0:T], NEG if d == 0 else s)
-            S[h, :, at:at + T] = s
-            top = jnp.maximum(s[:, :128], s[:, 128:])
-            M[h] = top if d == 0 else jnp.maximum(M[h], top)
+            best = None if 0 in ds else M[h]
+            for d in ds:
+                s = jnp.dot(qa[h], kT[d], preferred_element_type=F32)
+                at = (d % BLOCKS) * T
+                if d in (0, BLOCKS):
+                    seen = iota((T, T), 1) <= iota((T, T), 0)
+                    s = jnp.where(seen, s if d == 0 else S[h, :, 0:T], NEG if d == 0 else s)
+                S[h, :, at:at + T] = s
+                m = jnp.maximum(s[:, :128], s[:, 128:])
+                best = m if best is None else jnp.maximum(best, m)
+            M[h] = best
             return carry
 
         lax.fori_loop(0, HEADS, body, 0)
@@ -210,8 +216,7 @@
     for k in range(2, 5):
         arrive(k)
         handed(k - 2)
-        top(2 * k - 3)
-        top(2 * k)
+        top(2 * k - 3, 2 * k)
     handed(3)
     top(7)
 
@@ -237,6 +242,7 @@
         low = iota((CH, 128), 1) < 64
         for n in range(2):
             o = jnp.dot(Pm[n * 256:(n + 1) * 256, :], vx[...], preferred_element_type=F32)
+            o = o[:, :128]
             o = o / pltpu.roll(o, 64, 1)
             for i in range(2):
                 even, odd = o[i * 128:i * 128 + 64], o[i * 128 + 64:i * 128 + 128]
@@ -434,7 +440,7 @@
             pltpu.VMEM((F, D), BF16),
             pltpu.VMEM((BLOCKS + 1, KROWS, 128), BF16),
             pltpu.VMEM((BLOCKS + 1, 128, T), BF16),
-            pltpu.VMEM(((BLOCKS + 1) * T, 128), BF16),
+            pltpu.VMEM(((BLOCKS + 1) * T, 256), BF16),
             pltpu.VMEM((HEADS, T, 128), BF16),
             pltpu.VMEM((HEADS, T, BLOCKS * T), F32),
             pltpu.VMEM((HEADS, T, 128), F32),

time: 79.9 us -> 76.9 us (0.962)
  the two profiles are of different devices: /device:TPU:160 before, /device:TPU:224 now
where the time goes in v4:
time: 76.9 us; the launch traced here: 76.7 us
  Pallas kernels  73.1 us (95%)
  local copies, waits for them, and re-layouts  2.97 us (4%)
    pallas_call x1, Pallas kernels, body(): pl.pallas_call(kernel, out_shape=(jax.ShapeDtypeStruct((T, D), BF16), jax...  73.1 us
    unnamed x4, local copies, waits for them, and re-layouts  2.97 us

profile of v4, /device:TPU:224, one launch (start us, length us, event | category | flops | bytes accessed | tf_op | source)
XLA Modules:
  0.0 76.7 jit_solution(5427030678349353163)
XLA Ops:
  0.6 73.1 %block.1 = (bf16[256,2048]{1,0:T(8,128)(2,1)}, bf16[256,128]{1,0:T(8,128)(2,1)}) custom-call(bf16[256,2048]{1,0:T(8,128)(2,1)} %tok_h.1, s32[1,256]{1,0:T(1,128)} %bitcast.5, f32[1,2048]{1,0:T(1,128)} %bitcast.3, f32[1,2048]{1,0:T(1,128)} %bitcast.4, f32[2,64,128]{2,1,0:T(8,128)} %constant.4.clone.base_ref, f32[2,256,128]{2,1,0:T(8,128)} %constant.5.clone.inner_ref, ...), custom_call_target="tpu_custom_call" | custom-call | tf_op jit(solution)/shard_map/block/pallas_call | solution.py:424
  73.8 0.0 copy-start
  73.8 2.3 %copy.16 = bf16[256,2048]{1,0:T(8,128)(2,1)} copy(bf16[256,2048]{1,0:T(8,128)(2,1)} %get-tuple-element.4) | data formatting | bytes 2097152
  76.1 0.0 copy-done
  76.1 0.6 copy.17
Async XLA Ops:
  73.8 2.3 %copy-start = (bf16[256,128]{1,0:T(8,128)(2,1)S(1)}, bf16[256,128]{1,0:T(8,128)(2,1)}, u32[]{:S(2)}) copy-start(bf16[256,128]{1,0:T(8,128)(2,1)} %get-tuple-element.5) | copy-start | bytes 196612
